TPU v7x, 32 devices: a whole 2x2x4 slice. The times are simulated.
32 devices in a mesh: row: 8 (over z, y), col: 4 (over x, core).
Axes of the slice: x: 2, y: 2, z: 4, core: 2. Of those that a mesh axis runs over, the one named last changes fastest.
Arguments:
- latents: bfloat16 [4, 1152, 4096], P(None, 'col', 'row'), may hold values from -6 to 6
- cond: bfloat16 [4, 1, 1152], P(None, None, 'row'), may hold values from -6 to 6
- w_ada: bfloat16 [2, 1152, 6, 1152], P(None, 'row', None, 'col'), may hold values from -0.1875 to 0.1875
- b_ada: bfloat16 [2, 6, 1152], P(None, None, 'col'), may hold values from -3 to 3
- w_qkv: bfloat16 [2, 1152, 3, 1152], P(None, 'row', None, 'col'), may hold values from -0.1875 to 0.1875
- b_qv: bfloat16 [2, 2, 1152], P(None, None, 'col'), may hold values from -3 to 3
- w_out: bfloat16 [2, 1152, 1152], P(None, 'row', 'col'), may hold values from -0.5 to 0.5
- b_out: bfloat16 [2, 1152], P(None, 'col'), may hold values from -2 to 2
- w_fc1: bfloat16 [2, 1152, 4608], P(None, 'row', 'col'), may hold values from -0.1875 to 0.1875
- b_fc1: bfloat16 [2, 4608], P(None, 'col'), may hold values from -3 to 3
- w_fc2: bfloat16 [2, 1152, 4608], P(None, 'row', 'col'), may hold values from -0.09375 to 0.09375
- b_fc2: bfloat16 [2, 1152], P(None, 'col'), may hold values from -2 to 2
- cotangent: bfloat16 [4, 1152, 4096], P(None, 'col', 'row'), may hold values from -6 to 6
Outputs:
- output: bfloat16 [4, 1152, 4096], P(None, 'col', 'row')
- grad_latents: float32 [4, 1152, 4096], P(None, 'col', 'row')
- grad_cond: float32 [4, 1, 1152], P(None, None, 'row')
- grad_w_ada: float32 [2, 1152, 6, 1152], P(None, 'row', None, 'col')
- grad_b_ada: float32 [2, 6, 1152], P(None, None, 'col')
- grad_w_qkv: float32 [2, 1152, 3, 1152], P(None, 'row', None, 'col')
- grad_b_qv: float32 [2, 2, 1152], P(None, None, 'col')
- grad_w_out: float32 [2, 1152, 1152], P(None, 'row', 'col')
- grad_b_out: float32 [2, 1152], P(None, 'col')
- grad_w_fc1: float32 [2, 1152, 4608], P(None, 'row', 'col')
- grad_b_fc1: float32 [2, 4608], P(None, 'col')
- grad_w_fc2: float32 [2, 1152, 4608], P(None, 'row', 'col')
- grad_b_fc2: float32 [2, 1152], P(None, 'col')
All inputs are finite; a program needn't handle non-finite values.
Results may differ from a plain program's by a relative error of at most 0.03.
Values may be sent and summed in bfloat16 or wider, within the bound.
No kernel may reach another device: no remote copies, remote signals or barrier semaphores. Data moves between devices by JAX's collectives and lax.ppermute only.
A program may use at most 320 MiB of HBM per device.

v0:
```python
import jax
import jax.numpy as jnp
from jax import lax
from jax.sharding import PartitionSpec as P

D = 1152
HD = 72
P_SIZE = 256
NF = 16
epsilon = 1e-06


def gelu_tanh(value):
    return jax.nn.gelu(value, approximate=True)


def contract_rows(left, right):
    return lax.dot_general(
        left, right, (((0,), (0,)), ((), ())), preferred_element_type=jnp.float32
    )


def contract_last(left, right):
    return lax.dot_general(
        left, right, (((1,), (1,)), ((), ())), preferred_element_type=jnp.float32
    )


def gather_features(value):
    return lax.all_gather(value, "col", axis=1, tiled=True)


def feature_sums(partial_value):
    return lax.psum_scatter(partial_value, "col", scatter_dimension=1, tiled=True)


def row_totals(first, second):
    return lax.psum((first, second), "col")


def fold_product(left, weight):
    return jnp.dot(
        left, lax.all_gather(weight, "row", axis=0, tiled=True), preferred_element_type=jnp.float32
    )


def map_product(left, weight):
    return contract_last(left, lax.all_gather(weight, "row", axis=0, tiled=True))


def norm_forward(stream):
    first, second = row_totals(jnp.sum(stream, 1), jnp.sum(stream * stream, 1))
    row_mean = first / D
    inverse = lax.rsqrt(second / D - row_mean * row_mean + epsilon)
    return ((stream - row_mean[:, None]) * inverse[:, None], inverse)


def norm_backward(grad_normed, normed, inverse):
    first, second = row_totals(jnp.sum(grad_normed, 1), jnp.sum(grad_normed * normed, 1))
    return inverse[:, None] * (grad_normed - first[:, None] / D - normed * second[:, None] / D)


def spread(vector, groups, tokens):
    width = vector.shape[-1]
    return jnp.broadcast_to(vector[:, None, :], (groups, tokens // groups, width)).reshape(
        tokens, width
    )


def group_sum(value, groups):
    return jnp.sum(value.reshape(groups, -1, value.shape[-1]), 1)


def split_heads(value, layout):
    return value.reshape(layout + (value.shape[1] // HD, HD))


def attention_scores(query_split, key_split):
    return jnp.einsum(
        "sqehd,skehd->sehqk", query_split, key_split, preferred_element_type=jnp.float32
    ) * HD ** (-0.5)


def attend_forward(queries, key_heads, value_heads, layout):
    tokens, width = queries.shape
    scores = attention_scores(split_heads(queries, layout), split_heads(key_heads, layout))
    largest = jnp.max(scores, -1, keepdims=True)
    powered = jnp.exp(scores - largest)
    total = jnp.sum(powered, -1, keepdims=True)
    soft_weights = (powered / total).astype(jnp.bfloat16)
    attended = jnp.einsum(
        "sehqk,skehd->sqehd",
        soft_weights,
        split_heads(value_heads, layout),
        preferred_element_type=jnp.float32,
    )
    return (attended.reshape(tokens, width), largest + jnp.log(total))


def attend_backward(queries, key_heads, value_heads, log_total, grad_out, layout):
    tokens, width = queries.shape
    query_split = split_heads(queries, layout)
    key_split = split_heads(key_heads, layout)
    value_split = split_heads(value_heads, layout)
    grad_split = split_heads(grad_out, layout)
    soft_weights = jnp.exp(attention_scores(query_split, key_split) - log_total)
    grad_weights = jnp.einsum(
        "sqehd,skehd->sehqk", grad_split, value_split, preferred_element_type=jnp.float32
    )
    grad_scores = (
        soft_weights * (grad_weights - jnp.sum(grad_weights * soft_weights, -1, keepdims=True))
    ).astype(jnp.bfloat16)
    factor = HD ** (-0.5)
    grad_query = (
        jnp.einsum("sehqk,skehd->sqehd", grad_scores, key_split, preferred_element_type=jnp.float32)
        * factor
    )
    grad_keys = (
        jnp.einsum(
            "sehqk,sqehd->skehd", grad_scores, query_split, preferred_element_type=jnp.float32
        )
        * factor
    )
    grad_values = jnp.einsum(
        "sehqk,sqehd->skehd",
        soft_weights.astype(jnp.bfloat16),
        grad_split,
        preferred_element_type=jnp.float32,
    )
    return (
        grad_query.reshape(tokens, width),
        grad_keys.reshape(tokens, width),
        grad_values.reshape(tokens, width),
    )


def block_forward(stream, modulate, weights, groups, layout):
    w_qkv, b_qv, w_out, b_out, w_fc1, b_fc1, w_fc2, b_fc2, out_local = weights
    tokens, width = stream.shape
    pieces = [spread(modulate[:, column], groups, tokens) for column in range(6)]
    normed, inverse = norm_forward(stream)
    hidden = (normed * (1.0 + pieces[1]) + pieces[0]).astype(jnp.bfloat16)
    hidden_all = gather_features(hidden)
    qv_bias = b_qv.astype(jnp.float32)
    biases = jnp.concatenate([qv_bias[0], jnp.zeros((width,), jnp.float32), qv_bias[1]])
    projected = (fold_product(hidden_all, w_qkv) + biases).astype(jnp.bfloat16)
    queries = projected[:, :width]
    key_heads = projected[:, width : 2 * width]
    value_heads = projected[:, 2 * width :]
    attended, log_total = attend_forward(queries, key_heads, value_heads, layout)
    attended_low = attended.astype(jnp.bfloat16)
    branch = feature_sums(map_product(attended_low, w_out)) + b_out.astype(jnp.float32)
    middle = stream + pieces[2] * branch
    normed_two, inverse_two = norm_forward(middle)
    hidden_two = (normed_two * (1.0 + pieces[4]) + pieces[3]).astype(jnp.bfloat16)
    hidden_two_all = gather_features(hidden_two)
    preact = fold_product(hidden_two_all, w_fc1) + b_fc1.astype(jnp.float32)
    activated = gelu_tanh(preact).astype(jnp.bfloat16)
    branch_two = feature_sums(map_product(activated, w_fc2)) + b_fc2.astype(jnp.float32)
    result = middle + pieces[5] * branch_two
    kept = (
        normed,
        inverse,
        hidden_all,
        queries,
        key_heads,
        value_heads,
        log_total,
        attended_low,
        branch,
        normed_two,
        inverse_two,
        hidden_two_all,
        preact,
        activated,
        branch_two,
    )
    return (result, kept)


def block_backward(grad, kept, modulate, weights, groups, layout):
    (
        normed,
        inverse,
        hidden_all,
        queries,
        key_heads,
        value_heads,
        log_total,
        attended_low,
        branch,
        normed_two,
        inverse_two,
        hidden_two_all,
        preact,
        activated,
        branch_two,
    ) = kept
    w_qkv, b_qv, w_out, b_out, w_fc1, b_fc1, w_fc2, b_fc2, out_local = weights
    tokens, width = grad.shape
    pieces = [spread(modulate[:, column], groups, tokens) for column in range(6)]
    grad_branch_two = (pieces[5] * grad).astype(jnp.bfloat16)
    grad_two_all = gather_features(grad_branch_two)
    grad_activated = fold_product(grad_two_all, w_fc2)
    grad_preact = jax.vjp(gelu_tanh, preact)[1](grad_activated)[0].astype(jnp.bfloat16)
    grad_hidden_two = feature_sums(map_product(grad_preact, w_fc1))
    grad_middle = grad + norm_backward(grad_hidden_two * (1.0 + pieces[4]), normed_two, inverse_two)
    grad_branch = (pieces[2] * grad_middle).astype(jnp.bfloat16)
    grad_branch_all = gather_features(grad_branch)
    grad_attended = fold_product(grad_branch_all, w_out).astype(jnp.bfloat16)
    grad_query, grad_keys, grad_values = attend_backward(
        queries, key_heads, value_heads, log_total, grad_attended, layout
    )
    grad_mixed = jnp.concatenate([grad_query, grad_keys, grad_values], 1).astype(jnp.bfloat16)
    grad_hidden = feature_sums(map_product(grad_mixed, w_qkv))
    grad_stream = grad_middle + norm_backward(grad_hidden * (1.0 + pieces[1]), normed, inverse)
    modulate_grad = jnp.stack(
        [
            group_sum(grad_hidden, groups),
            group_sum(grad_hidden * normed, groups),
            group_sum(grad_middle * branch, groups),
            group_sum(grad_hidden_two, groups),
            group_sum(grad_hidden_two * normed_two, groups),
            group_sum(grad * branch_two, groups),
        ],
        1,
    )
    weight_grads = (
        contract_rows(hidden_all, grad_mixed),
        contract_rows(grad_branch_all, attended_low),
        contract_rows(hidden_two_all, grad_preact),
        contract_rows(grad_two_all, activated),
    )
    mixed_float = grad_mixed.astype(jnp.float32)
    bias_grads = (
        jnp.stack([jnp.sum(mixed_float[:, :width], 0), jnp.sum(mixed_float[:, 2 * width :], 0)]),
        jnp.sum(grad_branch.astype(jnp.float32), 0),
        jnp.sum(grad_preact.astype(jnp.float32), 0),
        jnp.sum(grad_branch_two.astype(jnp.float32), 0),
    )
    return (grad_stream, weight_grads, bias_grads, modulate_grad)


def to_positions(value, frames_dev, row_count, pos_block):
    tokens, width = value.shape
    shaped = value.reshape(frames_dev, row_count, pos_block, width)
    moved = lax.all_to_all(shaped, "row", split_axis=1, concat_axis=0, tiled=True)
    return moved.reshape(tokens, width)


def to_frames(value, frames_dev, row_count, pos_block):
    tokens, width = value.shape
    shaped = value.reshape(frames_dev * row_count, 1, pos_block, width)
    moved = lax.all_to_all(
        shaped.astype(jnp.bfloat16), "row", split_axis=0, concat_axis=1, tiled=True
    ).astype(shaped.dtype)
    return moved.reshape(tokens, width)


def shards(
    latents, cond, w_ada, b_ada, w_qkv, b_qv, w_out, b_out, w_fc1, b_fc1, w_fc2, b_fc2, cotangent
):
    batches, width, tokens = latents.shape
    lat_count = cond.shape[1]
    row_count = lax.axis_size("row")
    frames_dev = tokens // P_SIZE
    pos_block = tokens // (lat_count * NF)
    spatial = (frames_dev, P_SIZE, 1)
    temporal = (lat_count, NF, pos_block)
    cond_float = cond.astype(jnp.float32)
    cond_low = jax.nn.silu(cond_float).astype(jnp.bfloat16)
    mod_partial = jnp.einsum("mlr,brjk->mlbjk", cond_low, w_ada, preferred_element_type=jnp.float32)
    mod_all = lax.psum(mod_partial, "row") + b_ada.astype(jnp.float32)[None, None]
    qkv_weight, out_weight, fc1_weight, fc2_weight = (w_qkv, w_out, w_fc1, w_fc2)
    out_locals = [None, None]
    block_weights = [
        (
            qkv_weight[which].reshape(qkv_weight.shape[1], -1),
            b_qv[which],
            out_weight[which],
            b_out[which],
            fc1_weight[which],
            b_fc1[which],
            fc2_weight[which],
            b_fc2[which],
            out_locals[which],
        )
        for which in range(2)
    ]
    lat_here = lax.axis_index("row") * frames_dev // NF
    onehot = (jnp.arange(lat_count) == lat_here).astype(jnp.float32)
    outputs = []
    grad_inputs = []
    mod_grads = []
    weight_totals = None
    bias_totals = None
    for batch_index in range(batches):
        mod_batch = mod_all[batch_index]
        mod_space = lax.dynamic_slice_in_dim(mod_batch[:, 0], lat_here, 1, 0)
        mod_time = mod_batch[:, 1]
        first_out, kept_space = block_forward(
            latents[batch_index].T.astype(jnp.float32), mod_space, block_weights[0], 1, spatial
        )
        second_in = to_positions(first_out, frames_dev, row_count, pos_block)
        second_out, kept_time = block_forward(
            second_in, mod_time, block_weights[1], lat_count, temporal
        )
        outputs.append(
            to_frames(second_out, frames_dev, row_count, pos_block).astype(jnp.bfloat16).T
        )
        grad_top = to_positions(
            cotangent[batch_index].T.astype(jnp.float32), frames_dev, row_count, pos_block
        )
        grad_mid, weights_time, biases_time, mod_grad_time = block_backward(
            grad_top, kept_time, mod_time, block_weights[1], lat_count, temporal
        )
        grad_low = to_frames(grad_mid, frames_dev, row_count, pos_block)
        grad_first, weights_space, biases_space, mod_grad_space = block_backward(
            grad_low, kept_space, mod_space, block_weights[0], 1, spatial
        )
        grad_inputs.append(grad_first.T)
        mod_grads.append(jnp.stack([onehot[:, None, None] * mod_grad_space, mod_grad_time], 1))
        terms = tuple(
            (jnp.stack([weights_space[column], weights_time[column]]) for column in range(4))
        )
        bias_terms = tuple(
            (jnp.stack([biases_space[column], biases_time[column]]) for column in range(4))
        )
        terms = (
            lax.psum_scatter(
                terms[0].astype(jnp.bfloat16), "row", scatter_dimension=1, tiled=True
            ).astype(jnp.float32),
            lax.psum_scatter(
                terms[1].astype(jnp.bfloat16), "row", scatter_dimension=1, tiled=True
            ).astype(jnp.float32),
            lax.psum_scatter(
                terms[2].astype(jnp.bfloat16), "row", scatter_dimension=1, tiled=True
            ).astype(jnp.float32),
            lax.psum_scatter(
                terms[3].astype(jnp.bfloat16), "row", scatter_dimension=1, tiled=True
            ).astype(jnp.float32),
        )
        if weight_totals is None:
            weight_totals = terms
            bias_totals = bias_terms
        else:
            weight_totals = jax.tree.map(jnp.add, weight_totals, terms)
            bias_totals = jax.tree.map(jnp.add, bias_totals, bias_terms)
    mod_grad_all, grad_bias_qv, grad_bias_out, grad_bias_fc1, grad_bias_fc2 = lax.psum(
        (jnp.stack(mod_grads), bias_totals[0], bias_totals[1], bias_totals[2], bias_totals[3]),
        "row",
    )
    mod_grad_low = mod_grad_all.astype(jnp.bfloat16)
    grad_bias_ada = jnp.sum(mod_grad_low.astype(jnp.float32), (0, 1))
    grad_weight_ada = jnp.einsum(
        "mlr,mlbjk->brjk", cond_low, mod_grad_low, preferred_element_type=jnp.float32
    )
    cond_partial = jnp.einsum(
        "mlbjk,brjk->mlr", mod_grad_low, w_ada, preferred_element_type=jnp.float32
    )
    cond_total = lax.psum(cond_partial, "col")
    sigmoid_cond = jax.nn.sigmoid(cond_float)
    grad_condition = cond_total * sigmoid_cond * (1.0 + cond_float * (1.0 - sigmoid_cond))
    grad_weight_qkv = weight_totals[0].reshape(2, weight_totals[0].shape[1], 3, width)
    return (
        jnp.stack(outputs),
        jnp.stack(grad_inputs),
        grad_condition,
        grad_weight_ada,
        grad_bias_ada,
        grad_weight_qkv,
        grad_bias_qv,
        weight_totals[1],
        grad_bias_out,
        weight_totals[2],
        grad_bias_fc1,
        weight_totals[3],
        grad_bias_fc2,
    )


def solution(mesh):
    placed = (
        P(None, "col", "row"),
        P(None, None, "row"),
        P(None, "row", None, "col"),
        P(None, None, "col"),
        P(None, "row", None, "col"),
        P(None, None, "col"),
        P(None, "row", "col"),
        P(None, "col"),
        P(None, "row", "col"),
        P(None, "col"),
        P(None, "row", "col"),
        P(None, "col"),
        P(None, "col", "row"),
    )
    return jax.shard_map(
        shards,
        mesh=mesh,
        in_specs=placed,
        out_specs=(
            P(None, "col", "row"),
            P(None, "col", "row"),
            P(None, None, "row"),
            P(None, "row", None, "col"),
            P(None, None, "col"),
            P(None, "row", None, "col"),
            P(None, None, "col"),
            P(None, "row", "col"),
            P(None, "col"),
            P(None, "row", "col"),
            P(None, "col"),
            P(None, "row", "col"),
            P(None, "col"),
        ),
        check_vma=False,
    )
```

profile of v0, /device:TPU:0, one launch (start us, length us, event | category | flops | bytes accessed | tf_op | source)
XLA Modules:
  0.0 4143.3 jit_solution(4381274286340281583)
XLA Ops:
  12.1 39.9 psum.497
  64.3 34.9 all-gather
  187.7 43.8 %all-gather.113.cloned.1.call-done = bf16[1,1152,1152]{2,1,0:T(8,128)(2,1)} async-done(((bf16[1,144,1152]{2,1,0:T(8,128)(2,1)}), bf16[1,1152,1152]{2,1,0:T(8,128)(2,1)}) %all-gather.113.cloned.1.call-update) | async-done | bytes 2654224 | tf_op jit(solution)/shard_map/all_gather | solution.py:43
  254.9 52.5 %all-gather.115.cloned.1.call-done = bf16[1,1152,1152]{2,1,0:T(8,128)(2,1)} async-done(((bf16[1,144,1152]{2,1,0:T(8,128)(2,1)}), bf16[1,1152,1152]{2,1,0:T(8,128)(2,1)}) %all-gather.115.cloned.1.call-update) | async-done | bytes 2654224 | tf_op jit(solution)/shard_map/all_gather | solution.py:48
  402.4 34.4 all-gather.3
  509.7 37.8 all_to_all.228
  596.2 57.3 %all-gather.119.cloned.1.call-done = bf16[1,1152,1152]{2,1,0:T(8,128)(2,1)} async-done(((bf16[1,144,1152]{2,1,0:T(8,128)(2,1)}), bf16[1,1152,1152]{2,1,0:T(8,128)(2,1)}) %all-gather.119.cloned.1.call-update) | async-done | bytes 2654224 | tf_op jit(solution)/shard_map/all_gather | solution.py:48
  782.4 33.1 reduce-scatter.75.cloned.1.call-done
  877.6 33.1 reduce-scatter.77.cloned.1.call-done
  955.0 32.3 reduce-scatter.79.cloned.1.call-done
  1094.2 35.6 reduce-scatter.65.cloned.1.call-done
  1129.8 35.6 reduce-scatter.49.cloned.1.call-done
  1274.2 35.5 reduce-scatter.59.cloned.1.call-done
  1309.7 35.8 reduce-scatter.67.cloned.1.call-done
  1529.6 35.7 reduce-scatter.61.cloned.1.call-done
  1565.2 35.6 reduce-scatter.53.cloned.1.call-done
  1816.7 33.5 reduce-scatter.81.cloned.1.call-done
  1921.5 35.6 reduce-scatter.55.cloned.1.call-done
  2053.9 32.5 reduce-scatter.83.cloned.1.call-done
  2088.3 33.7 reduce-scatter.99.cloned.1.call-done
  2281.3 33.7 reduce-scatter.85.cloned.1.call-done
  2317.0 33.5 reduce-scatter.101.cloned.1.call-done
  2714.9 52.5 %reduce-scatter.115.cloned.1.call-done = bf16[2,144,1152]{2,1,0:T(8,128)(2,1)} async-done(((bf16[2,1152,1152]{2,1,0:T(8,128)(2,1)}), bf16[2,144,1152]{2,1,0:T(8,128)(2,1)}) %reduce-scatter.115.cloned.1.call-update) | async-done | bytes 663568 | tf_op jit(solution)/shard_map/reduce_scatter | solution.py:339
  2767.4 107.2 %reduce-scatter.117.cloned.1.call-done = bf16[2,144,1152]{2,1,0:T(8,128)(2,1)} async-done(((bf16[2,1152,1152]{2,1,0:T(8,128)(2,1)}), bf16[2,144,1152]{2,1,0:T(8,128)(2,1)}) %reduce-scatter.117.cloned.1.call-update) | async-done | bytes 663568 | tf_op jit(solution)/shard_map/reduce_scatter | solution.py:339
  2877.8 104.0 %reduce-scatter.105.cloned.1.call-done = bf16[2,144,1152]{2,1,0:T(8,128)(2,1)} async-done(((bf16[2,1152,1152]{2,1,0:T(8,128)(2,1)}), bf16[2,144,1152]{2,1,0:T(8,128)(2,1)}) %reduce-scatter.105.cloned.1.call-update) | async-done | bytes 663568 | tf_op jit(solution)/shard_map/reduce_scatter | solution.py:336
  2981.7 107.1 %reduce-scatter.109.cloned.1.call-done = bf16[2,144,1152]{2,1,0:T(8,128)(2,1)} async-done(((bf16[2,1152,1152]{2,1,0:T(8,128)(2,1)}), bf16[2,144,1152]{2,1,0:T(8,128)(2,1)}) %reduce-scatter.109.cloned.1.call-update) | async-done | bytes 663568 | tf_op jit(solution)/shard_map/reduce_scatter | solution.py:336
  3088.9 107.1 %reduce-scatter.107.cloned.1.call-done = bf16[2,144,1152]{2,1,0:T(8,128)(2,1)} async-done(((bf16[2,1152,1152]{2,1,0:T(8,128)(2,1)}), bf16[2,144,1152]{2,1,0:T(8,128)(2,1)}) %reduce-scatter.107.cloned.1.call-update) | async-done | bytes 663568 | tf_op jit(solution)/shard_map/reduce_scatter | solution.py:336
  3196.0 107.2 %reduce-scatter.111.cloned.1.call-done = bf16[2,144,1152]{2,1,0:T(8,128)(2,1)} async-done(((bf16[2,1152,1152]{2,1,0:T(8,128)(2,1)}), bf16[2,144,1152]{2,1,0:T(8,128)(2,1)}) %reduce-scatter.111.cloned.1.call-update) | async-done | bytes 663568 | tf_op jit(solution)/shard_map/reduce_scatter | solution.py:336
  3338.5 36.2 reduce-scatter.87.cloned.1.call-done
  3374.7 35.8 reduce-scatter.103.cloned.1.call-done
  3413.5 40.3 all-reduce.8
  3473.1 650.4 %all-reduce.27.cloned.1.call-done = (bf16[2,1152,864]{2,0,1:T(2,128)(2,1)}, bf16[2,1152,864]{2,0,1:T(2,128)(2,1)}, bf16[2,1152,864]{2,0,1:T(2,128)(2,1)}, bf16[2...) async-done(((bf16[2,1152,864]{2,0,1:T(2,128)(2,1)}, ...) | async-done | bytes 21233680
  (1738 shorter events, 1958.1 us)
Async XLA Ops:
  63.4 110.1 %reduce-scatter.41.cloned.1.call-start = ((), (), s32[]{:S(2)}) async-start(), calls=%async_computation.58 | async-start | bytes 2949120 | tf_op jit(solution)/shard_map/reduce_scatter | solution.py:34
  143.9 105.7 %all-gather.49.cloned.1.call-start = ((), (), s32[]{:S(2)}) async-start(), calls=%async_computation.59 | async-start | bytes 1474560 | tf_op jit(solution)/shard_map/all_gather | solution.py:30
  184.7 122.7 %all-gather.115.cloned.1.call-start = ((), (), s32[]{:S(2)}) async-start(), calls=%async_computation.131 | async-start | bytes 2985984 | tf_op jit(solution)/shard_map/all_gather | solution.py:48
  186.8 158.1 %reduce-scatter.43.cloned.1.call-start = ((), (), s32[]{:S(2)}) async-start(), calls=%async_computation.60 | async-start | bytes 2949120 | tf_op jit(solution)/shard_map/reduce_scatter | solution.py:34
  313.2 123.5 %all-gather.53.cloned.1.call-start = ((), (), s32[]{:S(2)}) async-start(), calls=%async_computation.62 | async-start | bytes 2322432 | tf_op jit(solution)/shard_map/all_gather | solution.py:43
  463.6 112.9 %all-gather.55.cloned.1.call-start = ((), (), s32[]{:S(2)}) async-start(), calls=%async_computation.64 | async-start | bytes 1474560 | tf_op jit(solution)/shard_map/all_gather | solution.py:30
  552.2 144.2 %reduce-scatter.73.cloned.1.call-start = ((), (), s32[]{:S(2)}) async-start(), calls=%async_computation.91 | async-start | bytes 2949120 | tf_op jit(solution)/shard_map/reduce_scatter | solution.py:34
  1054.8 110.6 %reduce-scatter.49.cloned.1.call-start = ((), (), s32[]{:S(2)}) async-start(), calls=%async_computation.67 | async-start | bytes 2949120 | tf_op jit(solution)/shard_map/reduce_scatter | solution.py:34
  1074.5 124.7 %all-gather.59.cloned.1.call-start = ((), (), s32[]{:S(2)}) async-start(), calls=%async_computation.68 | async-start | bytes 1474560 | tf_op jit(solution)/shard_map/all_gather | solution.py:30
  1227.5 118.0 %reduce-scatter.67.cloned.1.call-start = ((), (), s32[]{:S(2)}) async-start(), calls=%async_computation.85 | async-start | bytes 2949120 | tf_op jit(solution)/shard_map/reduce_scatter | solution.py:34
  1521.7 196.3 %all-gather.79.cloned.1.call-start = ((), (), s32[]{:S(2)}) async-start(), calls=%async_computation.88 | async-start | bytes 1474560 | tf_op jit(solution)/shard_map/all_gather | solution.py:30
  1618.4 105.0 %all-gather.105.cloned.1.call-start = ((), (), s32[]{:S(2)}) async-start(), calls=%async_computation.114 | async-start | bytes 1474560 | tf_op jit(solution)/shard_map/all_gather | solution.py:30
  1767.5 118.3 %reduce-scatter.63.cloned.1.call-start = ((), (), s32[]{:S(2)}) async-start(), calls=%async_computation.81 | async-start | bytes 2949120 | tf_op jit(solution)/shard_map/reduce_scatter | solution.py:34
  1773.4 148.1 %reduce-scatter.71.cloned.1.call-start = ((), (), s32[]{:S(2)}) async-start(), calls=%async_computation.89 | async-start | bytes 2949120 | tf_op jit(solution)/shard_map/reduce_scatter | solution.py:34
  1779.2 177.9 %reduce-scatter.55.cloned.1.call-start = ((), (), s32[]{:S(2)}) async-start(), calls=%async_computation.73 | async-start | bytes 2949120 | tf_op jit(solution)/shard_map/reduce_scatter | solution.py:34
  1785.1 191.6 %all-gather.99.cloned.1.call-start = ((), (), s32[]{:S(2)}) async-start(), calls=%async_computation.108 | async-start | bytes 1474560 | tf_op jit(solution)/shard_map/all_gather | solution.py:30
  1889.4 116.9 %all-gather.91.cloned.1.call-start = ((), (), s32[]{:S(2)}) async-start(), calls=%async_computation.100 | async-start | bytes 1474560 | tf_op jit(solution)/shard_map/all_gather | solution.py:30
  2235.8 114.7 %reduce-scatter.101.cloned.1.call-start = ((), (), s32[]{:S(2)}) async-start(), calls=%async_computation.119 | async-start | bytes 2949120 | tf_op jit(solution)/shard_map/reduce_scatter | solution.py:34
  2254.9 188.9 %all-gather.103.cloned.1.call-start = ((), (), s32[]{:S(2)}) async-start(), calls=%async_computation.112 | async-start | bytes 1474560 | tf_op jit(solution)/shard_map/all_gather | solution.py:30
  2368.7 136.1 %all-gather.111.cloned.1.call-start = ((), (), s32[]{:S(2)}) async-start(), calls=%async_computation.120 | async-start | bytes 1474560 | tf_op jit(solution)/shard_map/all_gather | solution.py:30
  2371.7 343.2 %reduce-scatter.113.cloned.1.call-start = ((), (), s32[]{:S(2)}) async-start(), calls=%async_computation.126 | async-start | bytes 5971968 | tf_op jit(solution)/shard_map/reduce_scatter | solution.py:339
  2380.7 334.3 %reduce-scatter.119.cloned.1.call-start = ((), (), s32[]{:S(2)}) async-start(), calls=%async_computation.129 | async-start | bytes 5971968 | tf_op jit(solution)/shard_map/reduce_scatter | solution.py:339
  2390.4 377.0 %reduce-scatter.115.cloned.1.call-start = ((), (), s32[]{:S(2)}) async-start(), calls=%async_computation.127 | async-start | bytes 5971968 | tf_op jit(solution)/shard_map/reduce_scatter | solution.py:339
  2400.2 474.4 %reduce-scatter.117.cloned.1.call-start = ((), (), s32[]{:S(2)}) async-start(), calls=%async_computation.128 | async-start | bytes 5971968 | tf_op jit(solution)/shard_map/reduce_scatter | solution.py:339
  2409.8 571.9 %reduce-scatter.105.cloned.1.call-start = ((), (), s32[]{:S(2)}) async-start(), calls=%async_computation.122 | async-start | bytes 5971968 | tf_op jit(solution)/shard_map/reduce_scatter | solution.py:336
  2418.1 670.7 %reduce-scatter.109.cloned.1.call-start = ((), (), s32[]{:S(2)}) async-start(), calls=%async_computation.124 | async-start | bytes 5971968 | tf_op jit(solution)/shard_map/reduce_scatter | solution.py:336
  2426.4 769.6 %reduce-scatter.107.cloned.1.call-start = ((), (), s32[]{:S(2)}) async-start(), calls=%async_computation.123 | async-start | bytes 5971968 | tf_op jit(solution)/shard_map/reduce_scatter | solution.py:336
  2434.9 868.3 %reduce-scatter.111.cloned.1.call-start = ((), (), s32[]{:S(2)}) async-start(), calls=%async_computation.125 | async-start | bytes 5971968 | tf_op jit(solution)/shard_map/reduce_scatter | solution.py:336
  2443.1 895.4 %reduce-scatter.95.cloned.1.call-start = ((), (), s32[]{:S(2)}) async-start(), calls=%async_computation.113 | async-start | bytes 2949120 | tf_op jit(solution)/shard_map/reduce_scatter | solution.py:34
  2457.5 917.2 %reduce-scatter.87.cloned.1.call-start = ((), (), s32[]{:S(2)}) async-start(), calls=%async_computation.105 | async-start | bytes 2949120 | tf_op jit(solution)/shard_map/reduce_scatter | solution.py:34
  2472.0 938.5 %reduce-scatter.103.cloned.1.call-start = ((), (), s32[]{:S(2)}) async-start(), calls=%async_computation.121 | async-start | bytes 2949120 | tf_op jit(solution)/shard_map/reduce_scatter | solution.py:34
  2518.6 1604.9 %all-reduce.27.cloned.1.call-start = ((), (), s32[]{:S(2)}) async-start(), calls=%async_computation.134 | async-start | bytes 47185920
  (471 other events, 21171.2 us)
Sparse Core Ops, SparseCore 0:
  79.3 50.9 all-gather.46
  176.4 55.0 all-gather.112
  252.4 55.0 all-gather.114
  347.7 60.2 all-gather.52
  496.8 61.8 all-gather.116
  598.4 55.0 all-gather.118
  698.7 33.0 reduce-scatter.46
  954.2 33.0 reduce-scatter.78
  1061.1 33.0 reduce-scatter.56
  1132.3 33.0 reduce-scatter.48
  1241.1 33.0 reduce-scatter.50
  1276.6 33.0 reduce-scatter.58
  1312.4 33.0 reduce-scatter.66
  1532.1 33.0 reduce-scatter.60
  1567.8 33.0 reduce-scatter.52
  1746.0 33.0 reduce-scatter.96
  1781.5 33.0 reduce-scatter.88
  1852.8 33.0 reduce-scatter.62
  2017.6 33.0 reduce-scatter.90
  2053.3 33.0 reduce-scatter.82
  2246.3 33.0 reduce-scatter.92
  2426.3 103.6 reduce-scatter.112
  2534.2 116.8 reduce-scatter.118
  2655.0 112.3 reduce-scatter.114
  2771.6 103.0 reduce-scatter.116
  2878.6 103.0 reduce-scatter.104
  2985.8 103.0 reduce-scatter.108
  3092.9 103.0 reduce-scatter.106
  3200.1 103.0 reduce-scatter.110
  3341.6 33.0 reduce-scatter.86
  3377.4 33.0 reduce-scatter.102
  3416.2 707.2 all-reduce.26
  (47 shorter events, 1036.3 us)
where the time goes:
time: 4160 us; the launch traced here: 4140 us
  waiting for transfers between devices  2730 us (66%)
  blocking collectives  403 us (10%)
  matrix products  393 us (9%)
  local copies, waits for them, and re-layouts  330 us (8%)
  other arithmetic  212 us (5%)
  starting transfers between devices  57.1 us (1%)
    reduce_scatter x32, waiting for transfers between devices, feature_sums(): lax.psum_scatter(partial_value, 'col', scatter_dimension=1, tiled=True)  917 us
    unnamed x80, waiting for transfers between devices  655 us
    reduce_scatter x4, waiting for transfers between devices, shards(): lax.psum_scatter(terms[2].astype(jnp.bfloat16), 'row', scatter_dimension=...  425 us
    all_gather x32, waiting for transfers between devices, gather_features(): return lax.all_gather(value, 'col', axis=1, tiled=True)  221 us
    reduce_scatter x4, waiting for transfers between devices, shards(): lax.psum_scatter(terms[3].astype(jnp.bfloat16), 'row', scatter_dimension=...  160 us
    dot_general x32, matrix products, fold_product(): jnp.dot(left, lax.all_gather(weight, 'row', axis=0, tiled=True), preferre...  143 us
    psum x15, blocking collectives, row_totals(): return lax.psum((first, second), 'col')  126 us
    dot_general x32, matrix products, contract_last(): lax.dot_general(left, right, (((1,), (1,)), ((), ())), preferred_element_...  116 us
  transfers between devices with their start and end apart: 90, of which 71 were waited for; matrix products, arithmetic and copies ran while one was open for 17% of the time, Pallas kernels for 0%

commit v1 on v0

--- a/solution.py
+++ b/solution.py
@@ -10,6 +10,19 @@
 epsilon = 1e-06
 
 
+def gather_around(array, axis, dim):
+    ways = lax.axis_size(axis)
+    up = [(d, (d + 1) % ways) for d in range(ways)]
+    down = [(d, (d - 1) % ways) for d in range(ways)]
+    earlier, later = ([array], [array])
+    for _ in range(ways // 2):
+        earlier.append(lax.ppermute(earlier[-1], axis, up))
+    for _ in range((ways - 1) // 2):
+        later.append(lax.ppermute(later[-1], axis, down))
+    line = jnp.concatenate([*earlier[::-1], *later[1:]], axis=dim)
+    return jnp.roll(line, (lax.axis_index(axis) - ways // 2) * array.shape[dim], axis=dim)
+
+
 def gelu_tanh(value):
     return jax.nn.gelu(value, approximate=True)
 
@@ -45,7 +58,7 @@
 
 
 def map_product(left, weight):
-    return contract_last(left, lax.all_gather(weight, "row", axis=0, tiled=True))
+    return contract_last(left, gather_around(weight, "row", 0))
 
 
 def norm_forward(stream):

time: 4160 us -> 4310 us (1.036)
  starting transfers between devices: 57.1 us -> 183 us
  waiting for transfers between devices: 2730 us -> 2680 us
  local copies, waits for them, and re-layouts: 330 us -> 378 us
    ppermute x0 -> x56, waiting for transfers between devices: none -> 261 us  [the longest x32 132 us: gather_around(): earlier.append(lax.ppermute(earlier[-1], axis, up))]
    ppermute x0 -> x56, starting transfers between devices: none -> 121 us  [the longest x24 92.5 us: gather_around(): later.append(lax.ppermute(later[-1], axis, down))]
    reduce_scatter x32, waiting for transfers between devices: 917 us -> 805 us  [feature_sums(): lax.psum_scatter(partial_value, 'col', scatter_dimension=1, tiled=True)]
    all_gather x2 -> x0, waiting for transfers between devices: 110 us -> none  [map_product(): lax.all_gather(weight, 'row', axis=0, tiled=True)]
    all_gather x32, waiting for transfers between devices: 221 us -> 142 us  [gather_features(): return lax.all_gather(value, 'col', axis=1, tiled=True)]
    unnamed x904 -> x991, local copies, waits for them, and re-layouts: 61 us -> 105 us
    all_to_all x7 -> x8, waiting for transfers between devices: 79.9 us -> 89.6 us  [to_frames(): lax.all_to_all(shaped.astype(jnp.bfloat16), 'row', split_axis=0, concat_a...]
  transfers between devices with their start and end apart: 90 -> 147, of which waited for: 71 -> 99; matrix products, arithmetic and copies ran while one was open for 17% -> 19% of each run, Pallas kernels for 0% -> 0%
where the time goes in v1:
time: 4310 us; the launch traced here: 4290 us
  waiting for transfers between devices  2680 us (62%)
  blocking collectives  390 us (9%)
  matrix products  387 us (9%)
  local copies, waits for them, and re-layouts  378 us (9%)
  other arithmetic  251 us (6%)
  starting transfers between devices  183 us (4%)
    reduce_scatter x32, waiting for transfers between devices, feature_sums(): lax.psum_scatter(partial_value, 'col', scatter_dimension=1, tiled=True)  805 us
    unnamed x80, waiting for transfers between devices  655 us
    reduce_scatter x4, waiting for transfers between devices, shards(): lax.psum_scatter(terms[2].astype(jnp.bfloat16), 'row', scatter_dimension=...  425 us
    reduce_scatter x4, waiting for transfers between devices, shards(): lax.psum_scatter(terms[3].astype(jnp.bfloat16), 'row', scatter_dimension=...  160 us
    dot_general x32, matrix products, fold_product(): jnp.dot(left, lax.all_gather(weight, 'row', axis=0, tiled=True), preferre...  142 us
    all_gather x32, waiting for transfers between devices, gather_features(): return lax.all_gather(value, 'col', axis=1, tiled=True)  142 us
    ppermute x32, waiting for transfers between devices, gather_around(): earlier.append(lax.ppermute(earlier[-1], axis, up))  132 us
    ppermute x24, waiting for transfers between devices, gather_around(): later.append(lax.ppermute(later[-1], axis, down))  129 us
  transfers between devices with their start and end apart: 147, of which 99 were waited for; matrix products, arithmetic and copies ran while one was open for 19% of the time, Pallas kernels for 0%

profile of v1, /device:TPU:0, one launch (start us, length us, event | category | flops | bytes accessed | tf_op | source)
XLA Modules:
  0.0 4289.7 jit_solution(4388474331109511098)
XLA Ops:
  12.1 39.9 psum.497
  433.9 32.6 reduce-scatter.45.cloned.1.call-done
  481.8 38.4 all_to_all.228
  625.8 34.0 all-gather.117.cloned.1.call-done
  763.3 36.3 all-gather.3
  842.9 33.7 reduce-scatter.75.cloned.1.call-done
  1040.1 34.5 all-gather.5
  1101.2 32.4 reduce-scatter.79.cloned.1.call-done
  1240.4 35.6 reduce-scatter.65.cloned.1.call-done
  1276.0 35.6 reduce-scatter.49.cloned.1.call-done
  1420.5 35.5 reduce-scatter.67.cloned.1.call-done
  1456.0 35.8 reduce-scatter.59.cloned.1.call-done
  1675.9 35.6 reduce-scatter.61.cloned.1.call-done
  1711.5 35.6 reduce-scatter.53.cloned.1.call-done
  1963.0 33.5 reduce-scatter.89.cloned.1.call-done
  2036.4 31.4 reduce-scatter.71.cloned.1.call-done
  2067.8 35.6 reduce-scatter.55.cloned.1.call-done
  2200.1 32.5 reduce-scatter.83.cloned.1.call-done
  2234.6 33.7 reduce-scatter.99.cloned.1.call-done
  2427.6 33.7 reduce-scatter.85.cloned.1.call-done
  2463.3 34.1 reduce-scatter.101.cloned.1.call-done
  2861.7 52.5 %reduce-scatter.115.cloned.1.call-done = bf16[2,144,1152]{2,1,0:T(8,128)(2,1)} async-done(((bf16[2,1152,1152]{2,1,0:T(8,128)(2,1)}), bf16[2,144,1152]{2,1,0:T(8,128)(2,1)}) %reduce-scatter.115.cloned.1.call-update) | async-done | bytes 663568 | tf_op jit(solution)/shard_map/reduce_scatter | solution.py:352
  2914.1 107.1 %reduce-scatter.117.cloned.1.call-done = bf16[2,144,1152]{2,1,0:T(8,128)(2,1)} async-done(((bf16[2,1152,1152]{2,1,0:T(8,128)(2,1)}), bf16[2,144,1152]{2,1,0:T(8,128)(2,1)}) %reduce-scatter.117.cloned.1.call-update) | async-done | bytes 663568 | tf_op jit(solution)/shard_map/reduce_scatter | solution.py:352
  3024.4 104.0 %reduce-scatter.105.cloned.1.call-done = bf16[2,144,1152]{2,1,0:T(8,128)(2,1)} async-done(((bf16[2,1152,1152]{2,1,0:T(8,128)(2,1)}), bf16[2,144,1152]{2,1,0:T(8,128)(2,1)}) %reduce-scatter.105.cloned.1.call-update) | async-done | bytes 663568 | tf_op jit(solution)/shard_map/reduce_scatter | solution.py:349
  3128.4 107.0 %reduce-scatter.109.cloned.1.call-done = bf16[2,144,1152]{2,1,0:T(8,128)(2,1)} async-done(((bf16[2,1152,1152]{2,1,0:T(8,128)(2,1)}), bf16[2,144,1152]{2,1,0:T(8,128)(2,1)}) %reduce-scatter.109.cloned.1.call-update) | async-done | bytes 663568 | tf_op jit(solution)/shard_map/reduce_scatter | solution.py:349
  3235.4 107.1 %reduce-scatter.107.cloned.1.call-done = bf16[2,144,1152]{2,1,0:T(8,128)(2,1)} async-done(((bf16[2,1152,1152]{2,1,0:T(8,128)(2,1)}), bf16[2,144,1152]{2,1,0:T(8,128)(2,1)}) %reduce-scatter.107.cloned.1.call-update) | async-done | bytes 663568 | tf_op jit(solution)/shard_map/reduce_scatter | solution.py:349
  3342.5 107.2 %reduce-scatter.111.cloned.1.call-done = bf16[2,144,1152]{2,1,0:T(8,128)(2,1)} async-done(((bf16[2,1152,1152]{2,1,0:T(8,128)(2,1)}), bf16[2,144,1152]{2,1,0:T(8,128)(2,1)}) %reduce-scatter.111.cloned.1.call-update) | async-done | bytes 663568 | tf_op jit(solution)/shard_map/reduce_scatter | solution.py:349
  3452.9 32.1 reduce-scatter.95.cloned.1.call-done
  3485.0 36.2 reduce-scatter.87.cloned.1.call-done
  3521.2 35.8 reduce-scatter.103.cloned.1.call-done
  3559.9 40.3 all-reduce.8
  3619.5 650.4 %all-reduce.27.cloned.1.call-done = (bf16[2,1152,864]{2,0,1:T(2,128)(2,1)}, bf16[2,1152,864]{2,0,1:T(2,128)(2,1)}, bf16[2,1152,864]{2,0,1:T(2,128)(2,1)}, bf16[2...) async-done(((bf16[2,1152,864]{2,0,1:T(2,128)(2,1)}, ...) | async-done | bytes 21233680
  (1954 shorter events, 2157.6 us)
Async XLA Ops:
  64.0 188.8 %reduce-scatter.41.cloned.1.call-start = ((), (), s32[]{:S(2)}) async-start(), calls=%async_computation.58 | async-start | bytes 2949120 | tf_op jit(solution)/shard_map/reduce_scatter | solution.py:47
  144.0 135.2 %all-gather.113.cloned.1.call-start = ((), (), s32[]{:S(2)}) async-start(), calls=%async_computation.130 | async-start | bytes 2985984 | tf_op jit(solution)/shard_map/all_gather | solution.py:56
  146.3 136.8 %all-gather.49.cloned.1.call-start = ((), (), s32[]{:S(2)}) async-start(), calls=%async_computation.59 | async-start | bytes 1474560 | tf_op jit(solution)/shard_map/all_gather | solution.py:43
  433.3 187.1 %all-gather.115.cloned.1.call-start = ((), (), s32[]{:S(2)}) async-start(), calls=%async_computation.131 | async-start | bytes 2985984 | tf_op jit(solution)/shard_map/all_gather | solution.py:56
  433.9 186.5 %all-gather.55.cloned.1.call-start = ((), (), s32[]{:S(2)}) async-start(), calls=%async_computation.64 | async-start | bytes 1474560 | tf_op jit(solution)/shard_map/all_gather | solution.py:43
  476.5 149.4 %all-gather.81.cloned.1.call-start = ((), (), s32[]{:S(2)}) async-start(), calls=%async_computation.90 | async-start | bytes 1474560 | tf_op jit(solution)/shard_map/all_gather | solution.py:43
  524.3 135.5 %all-gather.117.cloned.1.call-start = ((), (), s32[]{:S(2)}) async-start(), calls=%async_computation.132 | async-start | bytes 2985984 | tf_op jit(solution)/shard_map/all_gather | solution.py:56
  558.6 191.3 %reduce-scatter.73.cloned.1.call-start = ((), (), s32[]{:S(2)}) async-start(), calls=%async_computation.91 | async-start | bytes 2949120 | tf_op jit(solution)/shard_map/reduce_scatter | solution.py:47
  842.3 120.0 %all-gather.119.cloned.1.call-start = ((), (), s32[]{:S(2)}) async-start(), calls=%async_computation.133 | async-start | bytes 2985984 | tf_op jit(solution)/shard_map/all_gather | solution.py:56
  1220.7 124.7 %all-gather.59.cloned.1.call-start = ((), (), s32[]{:S(2)}) async-start(), calls=%async_computation.68 | async-start | bytes 1474560 | tf_op jit(solution)/shard_map/all_gather | solution.py:43
  1373.8 118.0 %reduce-scatter.59.cloned.1.call-start = ((), (), s32[]{:S(2)}) async-start(), calls=%async_computation.77 | async-start | bytes 2949120 | tf_op jit(solution)/shard_map/reduce_scatter | solution.py:47
  1668.1 195.9 %all-gather.79.cloned.1.call-start = ((), (), s32[]{:S(2)}) async-start(), calls=%async_computation.88 | async-start | bytes 1474560 | tf_op jit(solution)/shard_map/all_gather | solution.py:43
  1913.8 118.3 %reduce-scatter.63.cloned.1.call-start = ((), (), s32[]{:S(2)}) async-start(), calls=%async_computation.81 | async-start | bytes 2949120 | tf_op jit(solution)/shard_map/reduce_scatter | solution.py:47
  1919.7 148.1 %reduce-scatter.71.cloned.1.call-start = ((), (), s32[]{:S(2)}) async-start(), calls=%async_computation.89 | async-start | bytes 2949120 | tf_op jit(solution)/shard_map/reduce_scatter | solution.py:47
  1925.6 177.8 %reduce-scatter.55.cloned.1.call-start = ((), (), s32[]{:S(2)}) async-start(), calls=%async_computation.73 | async-start | bytes 2949120 | tf_op jit(solution)/shard_map/reduce_scatter | solution.py:47
  1931.4 191.6 %all-gather.99.cloned.1.call-start = ((), (), s32[]{:S(2)}) async-start(), calls=%async_computation.108 | async-start | bytes 1474560 | tf_op jit(solution)/shard_map/all_gather | solution.py:43
  2035.7 116.9 %all-gather.91.cloned.1.call-start = ((), (), s32[]{:S(2)}) async-start(), calls=%async_computation.100 | async-start | bytes 1474560 | tf_op jit(solution)/shard_map/all_gather | solution.py:43
  2382.1 115.3 %reduce-scatter.101.cloned.1.call-start = ((), (), s32[]{:S(2)}) async-start(), calls=%async_computation.119 | async-start | bytes 2949120 | tf_op jit(solution)/shard_map/reduce_scatter | solution.py:47
  2401.2 189.4 %all-gather.103.cloned.1.call-start = ((), (), s32[]{:S(2)}) async-start(), calls=%async_computation.112 | async-start | bytes 1474560 | tf_op jit(solution)/shard_map/all_gather | solution.py:43
  2515.6 136.0 %all-gather.111.cloned.1.call-start = ((), (), s32[]{:S(2)}) async-start(), calls=%async_computation.120 | async-start | bytes 1474560 | tf_op jit(solution)/shard_map/all_gather | solution.py:43
  2518.5 343.1 %reduce-scatter.113.cloned.1.call-start = ((), (), s32[]{:S(2)}) async-start(), calls=%async_computation.126 | async-start | bytes 5971968 | tf_op jit(solution)/shard_map/reduce_scatter | solution.py:352
  2527.5 334.2 %reduce-scatter.119.cloned.1.call-start = ((), (), s32[]{:S(2)}) async-start(), calls=%async_computation.129 | async-start | bytes 5971968 | tf_op jit(solution)/shard_map/reduce_scatter | solution.py:352
  2537.2 376.9 %reduce-scatter.115.cloned.1.call-start = ((), (), s32[]{:S(2)}) async-start(), calls=%async_computation.127 | async-start | bytes 5971968 | tf_op jit(solution)/shard_map/reduce_scatter | solution.py:352
  2547.0 474.2 %reduce-scatter.117.cloned.1.call-start = ((), (), s32[]{:S(2)}) async-start(), calls=%async_computation.128 | async-start | bytes 5971968 | tf_op jit(solution)/shard_map/reduce_scatter | solution.py:352
  2556.6 571.7 %reduce-scatter.105.cloned.1.call-start = ((), (), s32[]{:S(2)}) async-start(), calls=%async_computation.122 | async-start | bytes 5971968 | tf_op jit(solution)/shard_map/reduce_scatter | solution.py:349
  2564.9 670.5 %reduce-scatter.109.cloned.1.call-start = ((), (), s32[]{:S(2)}) async-start(), calls=%async_computation.124 | async-start | bytes 5971968 | tf_op jit(solution)/shard_map/reduce_scatter | solution.py:349
  2573.2 769.3 %reduce-scatter.107.cloned.1.call-start = ((), (), s32[]{:S(2)}) async-start(), calls=%async_computation.123 | async-start | bytes 5971968 | tf_op jit(solution)/shard_map/reduce_scatter | solution.py:349
  2581.7 868.0 %reduce-scatter.111.cloned.1.call-start = ((), (), s32[]{:S(2)}) async-start(), calls=%async_computation.125 | async-start | bytes 5971968 | tf_op jit(solution)/shard_map/reduce_scatter | solution.py:349
  2589.9 895.1 %reduce-scatter.95.cloned.1.call-start = ((), (), s32[]{:S(2)}) async-start(), calls=%async_computation.113 | async-start | bytes 2949120 | tf_op jit(solution)/shard_map/reduce_scatter | solution.py:47
  2604.3 916.8 %reduce-scatter.87.cloned.1.call-start = ((), (), s32[]{:S(2)}) async-start(), calls=%async_computation.105 | async-start | bytes 2949120 | tf_op jit(solution)/shard_map/reduce_scatter | solution.py:47
  2618.8 938.2 %reduce-scatter.103.cloned.1.call-start = ((), (), s32[]{:S(2)}) async-start(), calls=%async_computation.121 | async-start | bytes 2949120 | tf_op jit(solution)/shard_map/reduce_scatter | solution.py:47
  2665.7 1604.1 %all-reduce.27.cloned.1.call-start = ((), (), s32[]{:S(2)}) async-start(), calls=%async_computation.134 | async-start | bytes 47185920
  (545 other events, 22268.3 us)
Sparse Core Ops, SparseCore 0:
  79.3 53.0 all-gather.46
  178.6 82.1 all-gather.112
  327.4 61.1 all-gather.52
  468.8 61.8 all-gather.114
  532.3 51.0 all-gather.54
  604.7 55.0 all-gather.116
  712.6 34.8 reduce-scatter.46
  842.4 34.1 reduce-scatter.74
  878.6 77.0 all-gather.118
  988.6 33.0 reduce-scatter.76
  1100.4 33.0 reduce-scatter.78
  1207.3 33.0 reduce-scatter.56
  1278.5 33.0 reduce-scatter.48
  1387.4 33.0 reduce-scatter.50
  1458.7 33.0 reduce-scatter.58
  1642.8 33.0 reduce-scatter.68
  1714.1 33.0 reduce-scatter.52
  1927.8 33.0 reduce-scatter.80
  2070.3 33.0 reduce-scatter.54
  2163.9 33.0 reduce-scatter.90
  2199.6 33.0 reduce-scatter.82
  2235.2 33.0 reduce-scatter.98
  2573.8 103.9 reduce-scatter.112
  2682.0 116.2 reduce-scatter.118
  2802.3 111.7 reduce-scatter.114
  2918.3 102.9 reduce-scatter.116
  3025.3 103.0 reduce-scatter.104
  3132.4 102.9 reduce-scatter.108
  3239.4 103.0 reduce-scatter.106
  3346.6 103.0 reduce-scatter.110
  3523.9 33.0 reduce-scatter.102
  3562.7 707.1 all-reduce.26
  (47 shorter events, 1060.6 us)
